TPU v7x, 512 devices: a whole 4x4x16 slice. The times are simulated.
512 devices in a mesh: row: 32 (over y, z_hi, x), col: 16 (over z_lo, core).
Axes of the slice: x: 4, y: 4, z: 16 (z_hi: 2, z_lo: 8; z = z_hi * 8 + z_lo), core: 2. Of those that a mesh axis runs over, the one named last changes fastest.
Arguments:
- nodes: bfloat16 [2048, 512], P(('row', 'col')), may hold values from -50 to 50
- coords: float32 [3, 2048], P(None, ('row', 'col')), may hold values from -18 to 18
- atom_types: int32 [2048], P(('row', 'col')), may hold values from 0 to 29
- segment_ids: int32 [2048], P(('row', 'col')), may hold values from 0 to 1
- pair_mask: int32 [2048, 2048], P('row', 'col'), may hold values 0 or 1
- pair_bias: bfloat16 [64, 2048, 2048], P(None, 'row', 'col'), may hold values from -10 to 310
- ln_gain: float32 [512], replicated, may hold values from 0.1 to 1.9
- w_qkv: bfloat16 [512, 1536], replicated, may hold values from -0.25 to 0.25
- gauss_mul: float32 [60, 60], replicated, may hold values from 0.25 to 1.75
- gauss_add: float32 [60, 60], replicated, may hold values from -4 to 4
- gauss_mean: float32 [128], replicated, may hold values from 0 to 16
- gauss_width: float32 [128], replicated, may hold values from 0.5 to 2.5
- w_gauss: bfloat16 [128, 128], replicated, may hold values from -2 to 2
- w_heads: bfloat16 [128, 64], replicated, may hold values from -2 to 2
- w_coord1: bfloat16 [64, 64], replicated, may hold values from -0.75 to 0.75
- w_coord2: bfloat16 [64], replicated, may hold values from -0.75 to 0.75
Outputs:
- attended: bfloat16 [2048, 512], P(('row', 'col'))
- moved: float32 [3, 2048], P(None, ('row', 'col'))
All inputs are finite; a program needn't handle non-finite values. No bound on the sum of `pair_mask` on one device may be relied on, other than what follows from the above.
Results may differ from a plain program's by a relative error of at most 0.015.
Values may be sent and summed in bfloat16 or wider, within the bound.
A program may use at most 64 MiB of HBM per device.

v0:
```python
import math
import jax
import jax.numpy as jnp
from jax import lax
from jax.sharding import PartitionSpec as P

ln_epsilon = 1e-05
masked_fill = -1000000000.0
root_shift = 0.01


def combined_all(value, axis, join):
    pieces = jax.tree.map(lambda part: lax.all_gather(part, axis), value)
    head = jax.tree.map(lambda part: part[0], pieces)
    tail = jax.tree.map(lambda part: part[1:], pieces)
    total, _ = lax.scan(lambda total, piece: (join(total, piece), None), head, tail)
    return total


def layer_normed(nodes, ln_gain):
    features = nodes.astype(jnp.float32)
    row_mean = jnp.mean(features, axis=1, keepdims=True)
    centred = features - row_mean
    spread = jnp.mean(centred * centred, axis=1, keepdims=True)
    return (centred * lax.rsqrt(spread + ln_epsilon) * ln_gain[None, :]).astype(jnp.bfloat16)


def gaussians(expanded, gauss_mean, gauss_width):
    scaled = (expanded[None, :, :] - gauss_mean[:, None, None]) / gauss_width[:, None, None]
    norming = math.sqrt(2.0 * math.pi) * gauss_width[:, None, None]
    return (jnp.exp(-0.5 * scaled * scaled) / norming).astype(jnp.bfloat16)


def shards(
    nodes,
    coords,
    atom_types,
    segment_ids,
    pair_mask,
    pair_bias,
    ln_gain,
    w_qkv,
    gauss_mul,
    gauss_add,
    gauss_mean,
    gauss_width,
    w_gauss,
    w_heads,
    w_coord1,
    w_coord2,
):
    col_count = lax.axis_size("col")
    row_count = lax.axis_size("row")
    col_index = lax.axis_index("col")
    row_index = lax.axis_index("row")
    own_rows = nodes.shape[0]
    query_rows = own_rows * col_count
    key_cols = own_rows * row_count
    model_width = nodes.shape[1]
    head_count = pair_bias.shape[0]
    head_dim = model_width // head_count
    kind_count = gauss_mul.shape[0]
    all_atoms = own_rows * row_count * col_count
    highest = lax.Precision.HIGHEST
    normed = layer_normed(nodes, ln_gain)
    kinds = atom_types + kind_count // 2 * segment_ids
    own_table = jnp.concatenate([coords, kinds.astype(jnp.float32)[None, :]], axis=0)
    atom_table = lax.all_gather(own_table, ("row", "col"), axis=1, tiled=True)
    query_table = lax.dynamic_slice_in_dim(atom_table, row_index * query_rows, query_rows, 1)
    key_table = lax.dynamic_slice_in_dim(atom_table, col_index * key_cols, key_cols, 1)
    projected = jnp.dot(
        lax.all_gather(normed, "col", axis=0, tiled=True), w_qkv, preferred_element_type=jnp.float32
    ).astype(jnp.bfloat16)
    queries = projected[:, :model_width].reshape(query_rows, head_count, head_dim)
    row_keys = projected[:, model_width:]
    every_key = lax.all_gather(row_keys, "row", axis=0, tiled=True)
    col_keys = lax.dynamic_slice_in_dim(every_key, col_index * key_cols, key_cols, 0)
    keys_block = col_keys[:, :model_width].reshape(key_cols, head_count, head_dim)
    values_block = col_keys[:, model_width:].reshape(key_cols, head_count, head_dim)
    offsets = query_table[:3, :, None] - key_table[:3, None, :]
    distance = jnp.sqrt(jnp.sum(offsets * offsets, axis=0) + root_shift)
    kind_range = jnp.arange(kind_count, dtype=jnp.float32)
    query_onehot = (query_table[3][:, None] == kind_range[None, :]).astype(jnp.float32)
    key_onehot = (key_table[3][:, None] == kind_range[None, :]).astype(jnp.float32)
    both_tables = jnp.concatenate([gauss_mul, gauss_add], axis=1)
    row_lookup = jnp.dot(query_onehot, both_tables, precision=highest)
    scale_pair = jnp.dot(row_lookup[:, :kind_count], key_onehot.T, precision=highest)
    shift_pair = jnp.dot(row_lookup[:, kind_count:], key_onehot.T, precision=highest)
    expanded = scale_pair * distance + shift_pair
    features = gaussians(expanded, gauss_mean, gauss_width)
    hidden = jax.nn.gelu(
        jnp.einsum("kij,kl->lij", features, w_gauss, preferred_element_type=jnp.float32)
    ).astype(jnp.bfloat16)
    geometry = jnp.einsum("kij,kh->hij", hidden, w_heads, preferred_element_type=jnp.float32)
    affinity = jnp.einsum(
        "ihd,jhd->hij", queries, keys_block, preferred_element_type=jnp.float32
    ) / math.sqrt(head_dim)
    logits = pair_bias.astype(jnp.float32) + geometry + affinity
    pair_new = logits.astype(jnp.bfloat16)
    mixed = jax.nn.gelu(
        jnp.einsum("hij,hg->gij", pair_new, w_coord1, preferred_element_type=jnp.float32)
    ).astype(jnp.bfloat16)
    strength = jnp.einsum("gij,g->ij", mixed, w_coord2, preferred_element_type=jnp.float32)
    strength = jnp.where(pair_mask == 1, strength, 0.0)
    row_total = jnp.sum(strength, axis=1)
    pulled = jnp.dot(strength, key_table[:3].T, precision=highest)
    displace = (query_table[:3].T * row_total[:, None] - pulled) / all_atoms
    masked = jnp.where(pair_mask[None, :, :] == 1, logits, masked_fill)
    local_max = jnp.max(masked, axis=2)

    def join_partial(earlier, later):
        max_early, total_early, sums_early = earlier
        max_late, total_late, sums_late = later
        joined_max = jnp.maximum(max_early, max_late)
        factor_early = jnp.exp(max_early - joined_max)
        factor_late = jnp.exp(max_late - joined_max)
        joined_total = total_early * factor_early + total_late * factor_late
        row_span = sums_early.shape[0]
        joined_sums = (
            sums_early.reshape(row_span, head_count, head_dim) * factor_early.T[:, :, None]
            + sums_late.reshape(row_span, head_count, head_dim) * factor_late.T[:, :, None]
        )
        return (joined_max, joined_total, joined_sums.reshape(row_span, model_width))

    weights = jnp.exp(masked - local_max[:, :, None])
    denominator = jnp.sum(weights, axis=2)
    numerator = jnp.einsum(
        "hij,jhd->ihd",
        weights.astype(jnp.bfloat16),
        values_block,
        preferred_element_type=jnp.float32,
    ).reshape(query_rows, model_width)
    joined_max, joined_total, joined_sums = combined_all(
        (local_max, denominator, numerator), "col", join_partial
    )
    own_sums = lax.dynamic_slice_in_dim(joined_sums, col_index * own_rows, own_rows, 0)
    own_totals = lax.dynamic_slice_in_dim(joined_total, col_index * own_rows, own_rows, 1).T
    own_move = lax.psum_scatter(displace, "col", scatter_dimension=0, tiled=True)
    attended = (
        (own_sums.reshape(own_rows, head_count, head_dim) / own_totals[:, :, None])
        .reshape(own_rows, model_width)
        .astype(jnp.bfloat16)
    )
    moved = coords + own_move.T
    return (attended, moved)


def solution(mesh):
    in_specs = (
        P(("row", "col"), None),
        P(None, ("row", "col")),
        P(("row", "col")),
        P(("row", "col")),
        P("row", "col"),
        P(None, "row", "col"),
        P(),
        P(),
        P(),
        P(),
        P(),
        P(),
        P(),
        P(),
        P(),
        P(),
    )
    out_specs = (P(("row", "col"), None), P(None, ("row", "col")))
    return jax.shard_map(shards, mesh=mesh, in_specs=in_specs, out_specs=out_specs, check_vma=False)
```

profile of v0, /device:TPU:258, one launch (start us, length us, event | category | flops | bytes accessed | tf_op | source)
XLA Modules:
  0.0 1059.6 jit_solution(14597980474348112790)
XLA Ops:
  9.8 29.0 %all-gather.3 = bf16[16,4,512]{2,1,0:T(4,128)(2,1)S(1)} all-gather(bf16[1,4,512]{2,1,0:T(4,128)(2,1)S(1)} %fusion.73), channel_id=1, replica_groups=mesh['row'=32,'col'=16] {'col'}, dimensions={0}, use_global_device_ids=true | all-gather | bytes 69632 | tf_op jit(solution)/shard_map/all_gather | solution.py:72
  40.3 860.5 %all-gather.2 = f32[512,4,4]{2,1,0:T(4,128)S(1)} all-gather(f32[1,4,4]{2,1,0:T(4,128)S(1)} %bitcast.132), channel_id=1, replica_groups=mesh['row'=32,'col'=16] {'row','col'}, dimensions={0}, use_global_device_ids=true | all-gather | bytes 32832 | tf_op jit(solution)/shard_map/all_gather | solution.py:68
  902.0 1.0 fusion.89
  903.2 1.8 fusion.48
  905.1 6.5 fusion.25
  911.6 2.7 fusion.38
  914.4 2.3 select_reduce_fusion
  916.7 1.3 fusion.31
  919.7 1.3 dynamic-slice.2
  921.7 28.3 %all-gather.1 = f32[1024,64]{1,0:T(8,128)S(1)} all-gather(f32[64,64]{1,0:T(8,128)S(1)} %copy.113), channel_id=3, replica_groups=mesh['row'=32,'col'=16] {'col'}, dimensions={0}, use_global_device_ids=true | all-gather | bytes 278528 | tf_op jit(solution)/shard_map/all_gather | solution.py:13
  950.1 30.2 %all-gather = f32[1024,64]{1,0:T(8,128)S(1)} all-gather(f32[64,64]{1,0:T(8,128)S(1)} %copy.112), channel_id=2, replica_groups=mesh['row'=32,'col'=16] {'col'}, dimensions={0}, use_global_device_ids=true | all-gather | bytes 278528 | tf_op jit(solution)/shard_map/all_gather | solution.py:13
  980.6 47.1 %all-reduce = f32[64,3]{0,1:T(4,128)S(1)} all-reduce(f32[64,3]{0,1:T(4,128)S(1)} %fusion.39), channel_id=4, replica_groups=mesh['row'=32,'col'=16] {'col'}, use_global_device_ids=true, to_apply=%region_8.9.clone | all-reduce | flops 192 | bytes 1536
  1029.4 3.0 slice.79
  1032.4 19.2 %while.14 = (s32[]{:T(128)}, f32[64,64]{1,0:T(8,128)S(1)}, f32[64,64]{1,0:T(8,128)S(1)}, f32[64,512]{0,1:T(8,128)S(1)}, f32[15,64,64]{2,1,0:T(8,128)S(1)}, /*ind...) while((s32[]{:T(128)}, f32[64,64]{1,0:T(8,128)S(1)}, f32[64,64]{1,0:T(8,128)S(1)}, ...), condition=%wide.region_6.7_spmd, body=%wide.region_5.6_spmd.sunk | while | flops 126978 | bytes 1163369 | solution.py:16
  1032.5 0.9 constant_dynamic-slice_fusion.5
  1033.8 0.9 constant_dynamic-slice_fusion.5
  1035.0 0.9 constant_dynamic-slice_fusion.5
  1036.3 0.9 constant_dynamic-slice_fusion.5
  1037.6 0.9 constant_dynamic-slice_fusion.5
  1038.9 0.9 constant_dynamic-slice_fusion.5
  1040.2 0.9 constant_dynamic-slice_fusion.5
  1041.5 0.9 constant_dynamic-slice_fusion.5
  1042.7 0.9 constant_dynamic-slice_fusion.5
  1044.0 0.9 constant_dynamic-slice_fusion.5
  (159 shorter events, 19.4 us)
Async XLA Ops:
  7.2 31.7 %copy-start = (bf16[512,1536]{1,0:T(8,128)(2,1)S(1)}, bf16[512,1536]{1,0:T(8,128)(2,1)}, u32[]{:S(2)}) copy-start(bf16[512,1536]{1,0:T(8,128)(2,1)} %param.25) | copy-start | bytes 4718596
  7.2 32.9 %copy-start.10 = (s32[4]{0:T(128)S(1)}, s32[4]{0:T(128)}, u32[]{:S(2)}) copy-start(s32[4]{0:T(128)} %param.21) | copy-start | bytes 52
  7.2 32.9 %copy-start.9 = (s32[4]{0:T(128)S(1)}, s32[4]{0:T(128)}, u32[]{:S(2)}) copy-start(s32[4]{0:T(128)} %param.20) | copy-start | bytes 52
  7.2 32.9 %copy-start.5 = (f32[3,4]{1,0:T(4,128)S(1)}, f32[3,4]{1,0:T(4,128)}, u32[]{:S(2)}) copy-start(f32[3,4]{1,0:T(4,128)} %param.19) | copy-start | bytes 148
  7.2 894.8 %all-gather.7.cloned.1.call-start = ((), (), s32[]{:S(2)}) async-start(), calls=%async_computation | async-start | bytes 4325376 | tf_op jit(solution)/shard_map/all_gather | solution.py:76
  9.8 891.3 %copy-start.11 = (f32[128]{0:T(128)S(1)}, f32[128]{0:T(128)}, u32[]{:S(2)}) copy-start(f32[128]{0:T(128)} %param.29) | copy-start | bytes 1540
  9.8 891.3 %copy-start.2 = (f32[60,60]{1,0:T(8,128)S(1)}, f32[60,60]{1,0:T(8,128)}, u32[]{:S(2)}) copy-start(f32[60,60]{1,0:T(8,128)} %param.27) | copy-start | bytes 43204
  9.8 891.3 %copy-start.3 = (f32[60,60]{1,0:T(8,128)S(1)}, f32[60,60]{1,0:T(8,128)}, u32[]{:S(2)}) copy-start(f32[60,60]{1,0:T(8,128)} %param.26) | copy-start | bytes 43204
  40.0 988.4 %all-gather.9.cloned.1.call-start = ((), (), s32[]{:S(2)}) async-start(), calls=%async_computation.1 | async-start | bytes 2228224 | tf_op jit(solution)/shard_map/all_gather | solution.py:13
  900.8 4.2 copy-start.6
  900.8 4.2 copy-start.7
  900.8 4.2 copy-start.12
  905.1 6.5 copy-start.8
  905.1 6.5 copy-start.13
  911.6 2.7 copy-start.4
  914.3 2.5 copy-start.1
Sparse Core Ops, SparseCore 0:
  40.1 151.4 all-gather.6
  919.8 101.6 all-gather.8
where the time goes:
time: 1060 us
  blocking collectives  995 us (94%)
  local copies, waits for them, and re-layouts  24.8 us (2%)
  between operations  15 us (1%)
  matrix products  13.1 us (1%)
  other arithmetic  10.6 us (1%)
    all_gather x1, blocking collectives, shards(): atom_table = lax.all_gather(own_table, ('row', 'col'), axis=1, tiled=True)  860 us
    all_gather x2, blocking collectives, combined_all(): pieces = jax.tree.map(lambda part: lax.all_gather(part, axis), value)  58.6 us
    unnamed x1, blocking collectives  47.1 us
    all_gather x1, blocking collectives, shards(): lax.all_gather(normed, 'col', axis=0, tiled=True)  29 us
  transfers between devices with their start and end apart: 2, of which 0 were waited for; matrix products, arithmetic and copies ran while one was open for 0% of the time, Pallas kernels for 0%

commit v1 on v0

--- a/solution.py
+++ b/solution.py
@@ -1,12 +1,29 @@
+import functools
 import math
 import jax
 import jax.numpy as jnp
 from jax import lax
 from jax.sharding import PartitionSpec as P
+from jax.lax import all_to_all, axis_size
 
 ln_epsilon = 1e-05
 masked_fill = -1000000000.0
 root_shift = 0.01
+
+
+def write_the_leaves(inner_x, dim_i):
+    return jnp.concatenate(
+        all_to_all(
+            jnp.stack(axis_size(("row", "col")) * [inner_x]),
+            axis_name=("row", "col"),
+            split_axis=0,
+            concat_axis=0,
+        ),
+        axis=dim_i,
+    )
+
+
+_see_rounds = functools.partial(write_the_leaves, dim_i=1)
 
 
 def combined_all(value, axis, join):
@@ -65,7 +82,7 @@
     normed = layer_normed(nodes, ln_gain)
     kinds = atom_types + kind_count // 2 * segment_ids
     own_table = jnp.concatenate([coords, kinds.astype(jnp.float32)[None, :]], axis=0)
-    atom_table = lax.all_gather(own_table, ("row", "col"), axis=1, tiled=True)
+    atom_table = _see_rounds(own_table)
     query_table = lax.dynamic_slice_in_dim(atom_table, row_index * query_rows, query_rows, 1)
     key_table = lax.dynamic_slice_in_dim(atom_table, col_index * key_cols, key_cols, 1)
     projected = jnp.dot(

time: 1060 us -> 390 us (0.37)
  the two profiles are of different devices: /device:TPU:258 before, /device:TPU:1 now
where the time goes in v1:
time: 390 us; the launch traced here: 389 us
  blocking collectives  153 us (39%)
  waiting for transfers between devices  152 us (39%)
  local copies, waits for them, and re-layouts  28.7 us (7%)
  starting transfers between devices  15.5 us (4%)
  between operations  15 us (4%)
  matrix products  13.1 us (3%)
  other arithmetic  10.5 us (3%)
    all_gather x1, waiting for transfers between devices, shards(): every_key = lax.all_gather(row_keys, 'row', axis=0, tiled=True)  77.4 us
    all_to_all x1, waiting for transfers between devices, write_the_leaves(): all_to_all(jnp.stack(axis_size(('row', 'col')) * [inner_x]), axis_name=('...  74.5 us
    all_gather x2, blocking collectives, combined_all(): pieces = jax.tree.map(lambda part: lax.all_gather(part, axis), value)  71.1 us
    unnamed x1, blocking collectives  44.7 us
    all_gather x1, blocking collectives, shards(): lax.all_gather(normed, 'col', axis=0, tiled=True)  37.7 us
    dynamic_slice x30, local copies, waits for them, and re-layouts, combined_all(): lax.scan(lambda total, piece: (join(total, piece), None), head, tail)  15.6 us
    all_to_all x1, starting transfers between devices, write_the_leaves(): all_to_all(jnp.stack(axis_size(('row', 'col')) * [inner_x]), axis_name=('...  15.5 us
  transfers between devices with their start and end apart: 3, of which 2 were waited for; matrix products, arithmetic and copies ran while one was open for 2% of the time, Pallas kernels for 0%

profile of v1, /device:TPU:1, one launch (start us, length us, event | category | flops | bytes accessed | tf_op | source)
XLA Modules:
  0.0 389.1 jit_solution(3300917331694005998)
XLA Ops:
  9.8 37.7 %all-gather.2 = bf16[16,4,512]{2,1,0:T(4,128)(2,1)S(1)} all-gather(bf16[1,4,512]{2,1,0:T(4,128)(2,1)S(1)} %fusion.73), channel_id=1, replica_groups=mesh['row'=32,'col'=16] {'col'}, dimensions={0}, use_global_device_ids=true | all-gather | bytes 69632 | tf_op jit(solution)/shard_map/all_gather | solution.py:89
  48.7 1.1 stack.2
  49.8 15.5 %all-to-all-start = ((f32[512,4,4]{2,1,0:T(4,128)}), f32[512,4,4]{2,1,0:T(4,128)S(1)}, u32[]{:S(2)}, u32[]{:S(2)}) async-start(f32[512,4,4]{2,1,0:T(4,128)} %stack.2), calls=%async_computation | async-start | bytes 2097152 | tf_op jit(solution)/shard_map/all_to_all | solution.py:16
  65.5 74.5 %all-to-all-done = f32[512,4,4]{2,1,0:T(4,128)S(1)} async-done(((f32[512,4,4]{2,1,0:T(4,128)}), f32[512,4,4]{2,1,0:T(4,128)S(1)}, u32[]{:S(2)}, u32[]{:S(2)}) %all-to-all-start) | async-done | bytes 32800 | tf_op jit(solution)/shard_map/all_to_all | solution.py:16
  140.0 1.0 copy.99
  141.0 1.9 reshape.63
  144.0 77.4 %all-gather.6.cloned.1.call-done = bf16[2048,1024]{1,0:T(8,128)(2,1)} async-done(((bf16[64,1024]{1,0:T(8,128)(2,1)}), bf16[2048,1024]{1,0:T(8,128)(2,1)}) %all-gather.6.cloned.1.call-update) | async-done | bytes 4194320 | tf_op jit(solution)/shard_map/all_gather | solution.py:93
  221.4 1.0 fusion.89
  222.6 1.8 fusion.48
  224.5 6.5 %fusion.25 = f32[64,64,128]{2,0,1:T(8,128)} fusion(f32[64,64,128]{2,1,0:T(8,128)} %fusion.48, f32[128]{0:T(128)S(1)} %broadcast_multiply_fusion.1, f32[128]{0:T(128)S(1)} %copy-done.11, f32[128]{0:T(128)S(1)} %copy-done.12, f32[64,128]{1,0:T(8,128)S(1)} %convolution_add_fusion, bf16[64,64,128]{2,1,0:T(8,128)(2,1)} %param.23, ...), kind=kOutput, calls=%fused_computation.36 | convolution fusion | flops 420478976 | bytes 5326336 | tf_op jit(solution)/shard_map/kij,kh->hij/dot_general | solution.py:111
  231.0 2.7 fusion.38
  233.8 2.3 select_reduce_fusion
  236.2 1.3 fusion.31
  239.1 1.3 dynamic-slice
  241.2 40.3 %all-gather.1 = f32[1024,64]{1,0:T(8,128)S(1)} all-gather(f32[64,64]{1,0:T(8,128)S(1)} %copy.105), channel_id=3, replica_groups=mesh['row'=32,'col'=16] {'col'}, dimensions={0}, use_global_device_ids=true | all-gather | bytes 278528 | tf_op jit(solution)/shard_map/all_gather | solution.py:30
  281.5 30.8 %all-gather = f32[1024,64]{1,0:T(8,128)S(1)} all-gather(f32[64,64]{1,0:T(8,128)S(1)} %copy.104), channel_id=2, replica_groups=mesh['row'=32,'col'=16] {'col'}, dimensions={0}, use_global_device_ids=true | all-gather | bytes 278528 | tf_op jit(solution)/shard_map/all_gather | solution.py:30
  312.5 44.7 %all-reduce = f32[64,3]{0,1:T(4,128)S(1)} all-reduce(f32[64,3]{0,1:T(4,128)S(1)} %fusion.39), channel_id=4, replica_groups=mesh['row'=32,'col'=16] {'col'}, use_global_device_ids=true, to_apply=%region_8.9.clone | all-reduce | flops 192 | bytes 1536
  358.8 3.0 slice.79
  361.9 19.2 %while.14 = (s32[]{:T(128)}, f32[64,64]{1,0:T(8,128)S(1)}, f32[64,64]{1,0:T(8,128)S(1)}, f32[64,512]{0,1:T(8,128)S(1)}, f32[15,64,64]{2,1,0:T(8,128)S(1)}, /*ind...) while((s32[]{:T(128)}, f32[64,64]{1,0:T(8,128)S(1)}, f32[64,64]{1,0:T(8,128)S(1)}, ...), condition=%wide.region_6.7_spmd, body=%wide.region_5.6_spmd.sunk | while | flops 126978 | bytes 1163369 | solution.py:33
  361.9 0.9 constant_dynamic-slice_fusion.5
  363.2 0.9 constant_dynamic-slice_fusion.5
  364.5 0.9 constant_dynamic-slice_fusion.5
  365.8 0.9 constant_dynamic-slice_fusion.5
  367.1 0.9 constant_dynamic-slice_fusion.5
  (160 shorter events, 23.9 us)
Async XLA Ops:
  7.2 40.4 %copy-start = (bf16[512,1536]{1,0:T(8,128)(2,1)S(1)}, bf16[512,1536]{1,0:T(8,128)(2,1)}, u32[]{:S(2)}) copy-start(bf16[512,1536]{1,0:T(8,128)(2,1)} %param.25) | copy-start | bytes 4718596
  7.2 41.5 %copy-start.10 = (s32[4]{0:T(128)S(1)}, s32[4]{0:T(128)}, u32[]{:S(2)}) copy-start(s32[4]{0:T(128)} %param.21) | copy-start | bytes 52
  7.2 41.5 %copy-start.9 = (s32[4]{0:T(128)S(1)}, s32[4]{0:T(128)}, u32[]{:S(2)}) copy-start(s32[4]{0:T(128)} %param.20) | copy-start | bytes 52
  7.2 41.5 %copy-start.5 = (f32[3,4]{1,0:T(4,128)S(1)}, f32[3,4]{1,0:T(4,128)}, u32[]{:S(2)}) copy-start(f32[3,4]{1,0:T(4,128)} %param.19) | copy-start | bytes 148
  7.2 214.2 %all-gather.6.cloned.1.call-start = ((), (), s32[]{:S(2)}) async-start(), calls=%async_computation.1 | async-start | bytes 4325376 | tf_op jit(solution)/shard_map/all_gather | solution.py:93
  48.0 17.6 %copy-start.11 = (f32[128]{0:T(128)S(1)}, f32[128]{0:T(128)}, u32[]{:S(2)}) copy-start(f32[128]{0:T(128)} %param.29) | copy-start | bytes 1540
  49.8 90.2 %all-to-all-start = ((f32[512,4,4]{2,1,0:T(4,128)}), f32[512,4,4]{2,1,0:T(4,128)S(1)}, u32[]{:S(2)}, u32[]{:S(2)}) async-start(f32[512,4,4]{2,1,0:T(4,128)} %stack.2), calls=%async_computation | async-start | bytes 2097152 | tf_op jit(solution)/shard_map/all_to_all | solution.py:16
  65.3 77.9 %copy-start.2 = (f32[60,60]{1,0:T(8,128)S(1)}, f32[60,60]{1,0:T(8,128)}, u32[]{:S(2)}) copy-start(f32[60,60]{1,0:T(8,128)} %param.27) | copy-start | bytes 43204
  65.3 77.9 %copy-start.3 = (f32[60,60]{1,0:T(8,128)S(1)}, f32[60,60]{1,0:T(8,128)}, u32[]{:S(2)}) copy-start(f32[60,60]{1,0:T(8,128)} %param.26) | copy-start | bytes 43204
  65.3 292.5 %all-gather.8.cloned.1.call-start = ((), (), s32[]{:S(2)}) async-start(), calls=%async_computation.2 | async-start | bytes 2228224 | tf_op jit(solution)/shard_map/all_gather | solution.py:30
  142.9 81.5 %copy-start.6 = (bf16[128,128]{1,0:T(8,128)(2,1)S(1)}, bf16[128,128]{1,0:T(8,128)(2,1)}, u32[]{:S(2)}) copy-start(bf16[128,128]{1,0:T(8,128)(2,1)} %param.30) | copy-start | bytes 98308
  142.9 81.5 %copy-start.7 = (bf16[128,64]{0,1:T(8,128)(2,1)S(1)}, bf16[128,64]{0,1:T(8,128)(2,1)}, u32[]{:S(2)}) copy-start(bf16[128,64]{0,1:T(8,128)(2,1)} %param.31) | copy-start | bytes 49156
  142.9 81.5 %copy-start.12 = (f32[128]{0:T(128)S(1)}, f32[128]{0:T(128)}, u32[]{:S(2)}) copy-start(f32[128]{0:T(128)} %param.28) | copy-start | bytes 1540
  224.5 6.5 %copy-start.8 = (bf16[64,64]{1,0:T(8,128)(2,1)S(1)}, bf16[64,64]{1,0:T(8,128)(2,1)}, u32[]{:S(2)}) copy-start(bf16[64,64]{1,0:T(8,128)(2,1)} %param.32) | copy-start | bytes 24580
  224.5 6.5 %copy-start.13 = (bf16[64]{0:T(256)(128)(2,1)S(1)}, bf16[64]{0:T(256)(128)(2,1)}, u32[]{:S(2)}) copy-start(bf16[64]{0:T(256)(128)(2,1)} %param.33) | copy-start | bytes 388
  231.0 2.7 copy-start.4
  233.7 2.5 copy-start.1
Sparse Core Ops, SparseCore 0:
  48.8 172.5 all-gather.5
  239.2 104.8 all-gather.7
